TPU v7x, 32 devices: a whole 2x2x4 slice. The times are simulated.
32 devices in a mesh: rows: 4 (over z), coarse: 4 (over x, core), fine: 2 (over y).
Axes of the slice: x: 2, y: 2, z: 4, core: 2. Of those that a mesh axis runs over, the one named last changes fastest.
Arguments:
- eigvecs: bfloat16 [2048, 4096], P('rows', ('coarse', 'fine')), may hold values from -6 to 6
- perm: int32 [4096], P(('coarse', 'fine')), may hold values from 0 to 511, as said below
- counts: int32 [8], replicated, may hold values from 1 to 256, as said below
- poles: float32 [4096], replicated, may hold values from 0 to 4096, as said below
- weights: float32 [4096], replicated, may hold values from -10 to 10, as said below
- roots: float32 [4096], P(('coarse', 'fine')), may hold values from 0 to 4096, as said below
Outputs:
- merged: bfloat16 [2048, 4096], P('rows', ('coarse', 'fine'))
Inputs may be any that keep to these rules, and one draw needn't show every extreme that they name: `perm`: each aligned block of 512 entries is a permutation of 0 to 511. `counts`: at least one device has exactly 256. Every entry of poles lies 0.2 or more away from every entry of roots. `weights`: magnitudes 0.1 or more. `roots`: every entry lies 0.2 or more away from every entry of poles.
All inputs are finite; a program needn't handle non-finite values.
Results may differ from a plain program's by a relative error of at most 0.0027.
Values may be sent and summed in bfloat16 or wider, within the bound.
A program may use at most 64 MiB of HBM per device.

v0:
```python
import jax
import jax.numpy as jnp
from jax import lax
from jax.sharding import PartitionSpec as P

UNDEF_MOST = 256


def per_device(eigvecs, perm, counts, poles, weights, roots):
    columns_dev = eigvecs.shape[1]
    live_width = UNDEF_MOST
    device_total = counts.shape[0]
    n_fine = lax.axis_size("fine")
    device_ids = jnp.arange(device_total, dtype=jnp.int32)
    my_device = lax.axis_index("coarse") * n_fine + lax.axis_index("fine")
    my_count = jnp.sum(jnp.where(device_ids == my_device, counts, 0))
    column_ids = jnp.arange(columns_dev, dtype=jnp.int32)
    selector = (column_ids[:, None] == perm[None, :]).astype(jnp.bfloat16)
    permuted = jnp.dot(eigvecs, selector, preferred_element_type=jnp.float32).astype(jnp.bfloat16)
    own_roots = roots[:live_width]
    outgoing = permuted[:, :live_width]
    within = jnp.arange(live_width, dtype=jnp.int32)
    alive = within[None, :] < counts[:, None]
    factor_table = jnp.where(alive, weights.reshape(device_total, columns_dev)[:, :live_width], 0.0)
    pole_table = poles.reshape(device_total, columns_dev)[:, :live_width]
    factor_flat = factor_table.reshape(-1)
    pole_flat = pole_table.reshape(-1)
    panel_piece = lax.all_gather(outgoing, ("coarse", "fine"), axis=1, tiled=True)
    cauchy = factor_flat[:, None] / (pole_flat[:, None] - own_roots[None, :])
    summed = jnp.dot(panel_piece, cauchy.astype(jnp.bfloat16), preferred_element_type=jnp.float32)
    summed, squares = (summed, jnp.sum(cauchy * cauchy, axis=0))
    updated = summed / jnp.sqrt(squares)[None, :]
    retain = within < my_count
    leading = jnp.where(retain[None, :], updated, outgoing.astype(jnp.float32)).astype(jnp.bfloat16)
    return jnp.concatenate([leading, permuted[:, live_width:]], axis=1)


def solution(mesh):
    in_specs = (
        P("rows", ("coarse", "fine")),
        P(("coarse", "fine")),
        P(),
        P(),
        P(),
        P(("coarse", "fine")),
    )
    out_specs = P("rows", ("coarse", "fine"))
    return jax.shard_map(
        per_device, mesh=mesh, in_specs=in_specs, out_specs=out_specs, check_vma=False
    )
```

profile of v0, /device:TPU:0, one launch (start us, length us, event | category | flops | bytes accessed | tf_op | source)
XLA Modules:
  0.0 51.0 jit_solution(3918311433402058479)
XLA Ops:
  6.5 0.0 copy-start
  6.5 0.0 copy-start.4
  6.5 0.0 copy-start.1
  6.5 0.0 copy-start.2
  6.5 0.0 copy-start.3
  6.5 0.0 all-gather.2.cloned.1.call-start
  6.6 1.0 %copy-done = bf16[512,512]{1,0:T(8,128)(2,1)S(1)} copy-done((bf16[512,512]{1,0:T(8,128)(2,1)S(1)}, bf16[512,512]{1,0:T(8,128)(2,1)}, u32[]{:S(2)}) %copy-start) | copy-done | bytes 524312
  7.6 1.2 %fusion.2 = bf16[512,512]{0,1:T(8,128)(2,1)S(1)} fusion(bf16[512,512]{1,0:T(8,128)(2,1)S(1)} %copy-done, s32[512]{0:T(512)} %param.7), kind=kOutput, calls=%fused_computation.6 | convolution fusion | flops 269221888 | bytes 1050624 | tf_op jit(solution)/shard_map/dot_general | solution.py:19
  8.8 0.7 %fusion.13 = (bf16[512,256]{0,1:T(8,128)(2,1)}, bf16[512,256]{0,1:T(8,128)(2,1)S(1)}) fusion(bf16[512,512]{0,1:T(8,128)(2,1)S(1)} %fusion.2), kind=kLoop, calls=%fused_computation.22 | loop fusion | bytes 1048576 | tf_op jit(solution)/shard_map/slice | solution.py:21
  9.5 0.0 all-gather.2.cloned.1.call-update
  9.5 0.0 copy-done.4
  9.5 0.0 copy-done.1
  9.6 0.0 copy-done.2
  9.6 0.0 copy-done.3
  9.6 0.1 fusion.11
  9.7 0.7 %multiply_reduce_fusion = f32[256]{0:T(256)S(1)} fusion(f32[256]{0:T(256)S(1)} %slice.18, f32[2048]{0:T(1024)S(1)} %bitcast.10, f32[2048]{0:T(1024)S(1)} %bitcast.12), kind=kLoop, calls=%fused_computation | loop fusion | flops 2096896 | bytes 18432 | tf_op jit(solution)/shard_map/reduce_sum | solution.py:31
  10.4 0.7 %fusion.12 = s32[]{:T(128)} fusion(s32[8]{0:T(128)S(1)} %copy-done.3, s32[]{:T(128)S(6)} %add.3), kind=kLoop, calls=%fused_computation.21 | loop fusion | flops 23 | bytes 40 | tf_op jit(solution)/shard_map/reduce_sum | solution.py:16
  11.1 0.6 %iota_compare_fusion.2 = pred[256]{0:T(512)(128)(4,1)S(1)} fusion(s32[]{:T(128)} %fusion.12), kind=kLoop, calls=%fused_computation.20 | loop fusion | flops 256 | bytes 260 | tf_op jit(solution)/shard_map/lt | solution.py:33
  11.8 28.4 %all-gather.2.cloned.1.call-done = bf16[512,2048]{0,1:T(8,128)(2,1)} async-done(((bf16[512,256]{0,1:T(8,128)(2,1)}), bf16[512,2048]{0,1:T(8,128)(2,1)}) %all-gather.2.cloned.1.call-update) | async-done | bytes 2097168 | tf_op jit(solution)/shard_map/all_gather | solution.py:28
  40.2 3.0 %fusion.3 = bf16[512,256]{0,1:T(8,128)(2,1)S(1)} fusion(bf16[512,2048]{0,1:T(8,128)(2,1)} %all-gather.2.cloned.1.call-done, f32[256]{0:T(256)S(1)} %slice.18, f32[2048]{0:T(1024)S(1)} %bitcast.11, f32[2048]{0:T(1024)S(1)} %bitcast.13, f32[256]{0:T(256)S(1)} %sqrt.7, pred[256]{0:T(512)(128)(4,1)S(1)} %iota_compare_fusion.2, bf16[512,512]{0,1:T(8,128)(2,1)S(1)} %fusion.2), kind=kOutput, calls=%fused_computation.7 | convolution fusion | flops 538968064 | bytes 2640128 | tf_op jit(solution)/shard_map/dot_general | solution.py:30
  43.2 1.0 %copy.8 = bf16[512,512]{1,0:T(8,128)(2,1)} copy(bf16[512,512]{0,1:T(8,128)(2,1)S(1)} %pad_maximum_fusion) | data formatting | bytes 1048576 | tf_op jit(solution)/shard_map/concatenate | solution.py:35
  (8 shorter events, 0.1 us)
Async XLA Ops:
  6.5 1.0 %copy-start = (bf16[512,512]{1,0:T(8,128)(2,1)S(1)}, bf16[512,512]{1,0:T(8,128)(2,1)}, u32[]{:S(2)}) copy-start(bf16[512,512]{1,0:T(8,128)(2,1)} %param.6) | copy-start | bytes 1572868
  6.5 3.0 %copy-start.4 = (f32[512]{0:T(512)S(1)}, f32[512]{0:T(512)}, u32[]{:S(2)}) copy-start(f32[512]{0:T(512)} %param.11) | copy-start | bytes 6148
  6.5 3.0 %copy-start.1 = (f32[4096]{0:T(1024)S(1)}, f32[4096]{0:T(1024)}, u32[]{:S(2)}) copy-start(f32[4096]{0:T(1024)} %param.9) | copy-start | bytes 49156
  6.5 3.0 %copy-start.2 = (f32[4096]{0:T(1024)S(1)}, f32[4096]{0:T(1024)}, u32[]{:S(2)}) copy-start(f32[4096]{0:T(1024)} %param.10) | copy-start | bytes 49156
  6.5 3.1 %copy-start.3 = (s32[8]{0:T(128)S(1)}, s32[8]{0:T(128)}, u32[]{:S(2)}) copy-start(s32[8]{0:T(128)} %param.8) | copy-start | bytes 100
  6.5 33.6 %all-gather.2.cloned.1.call-start = ((), (), s32[]{:S(2)}) async-start(), calls=%async_computation | async-start | bytes 2359296 | tf_op jit(solution)/shard_map/all_gather | solution.py:28
Sparse Core Ops, SparseCore 0:
  9.6 30.4 all-gather.1
where the time goes:
time: 51.2 us; the launch traced here: 51 us
  waiting for transfers between devices  28.4 us (55%)
  between operations  13.5 us (26%)
  matrix products  4.14 us (8%)
  local copies, waits for them, and re-layouts  2.77 us (5%)
  other arithmetic  2.12 us (4%)
    all_gather x1, waiting for transfers between devices, per_device(): lax.all_gather(outgoing, ('coarse', 'fine'), axis=1, tiled=True)  28.4 us
    dot_general x1, matrix products, per_device(): jnp.dot(panel_piece, cauchy.astype(jnp.bfloat16), preferred_element_type=...  2.97 us
    dot_general x1, matrix products, per_device(): jnp.dot(eigvecs, selector, preferred_element_type=jnp.float32)  1.17 us
  transfers between devices with their start and end apart: 1, of which 1 were waited for; matrix products, arithmetic and copies ran while one was open for 4% of the time, Pallas kernels for 0%

commit v1 on v0

v1 whole, which is shorter than its diff:
```python
import functools

import jax
import jax.numpy as jnp
from jax import lax
from jax.experimental import pallas as pl
from jax.experimental.pallas import tpu as pltpu
from jax.sharding import PartitionSpec as P

UNDEF_MOST = 256
LANES = 128
CORES = 2
MESH = pl.DeviceIdType.MESH


def repeat(total, body):
    if total <= 8:
        for i in range(total):
            body(i)
    else:
        lax.fori_loop(0, total, lambda i, c: (body(i), c)[1], 0)


def merge_kernel(
    n_coarse, n_fine, pieces, eig_hbm, perm_hbm, counts_hbm, poles_hbm, weights_hbm, roots_hbm, out_hbm,
    eig, perm, counts, poles, weights, roots, select, panel, cauchy, total, rest, lead,
    in_sem, small_sem, out_sem, rest_sem, recv_sem, own_sem, partner_sem, cross_sem,
):
    rows, columns = eig.shape
    live = UNDEF_MOST
    device_total = n_coarse * n_fine
    n_x = n_coarse // CORES
    size = rows // pieces
    coarse = lax.axis_index("coarse")
    fine = lax.axis_index("fine")
    x = coarse // CORES
    core = lax.rem(coarse, CORES)
    other_core = 1 - core

    def owner_of(px, pc, pf):
        return (px * CORES + pc) * n_fine + pf

    def device_of(px, pc, pf):
        return {"coarse": px * CORES + pc, "fine": pf}

    me = owner_of(x, core, fine)
    x_of = lambda i: lax.rem(x + 1 + i, n_x)
    f_of = lambda j: lax.rem(fine + 1 + j, n_fine)
    partner = device_of(x, other_core, fine)

    barrier = pltpu.get_barrier_semaphore()
    pl.semaphore_signal(barrier, inc=1, device_id=partner, device_id_type=MESH)
    for i in range(n_x - 1):
        pl.semaphore_signal(barrier, inc=1, device_id=device_of(x_of(i), core, fine), device_id_type=MESH)
    for j in range(n_fine - 1):
        pl.semaphore_signal(barrier, inc=1, device_id=device_of(x, core, f_of(j)), device_id_type=MESH)

    perm_in = pltpu.make_async_copy(perm_hbm, perm, small_sem.at[0])
    perm_in.start()
    eig_in = []
    for k in range(pieces):
        part = pl.ds(k * size, size)
        copy = pltpu.make_async_copy(eig_hbm.at[part], eig.at[part], in_sem.at[k])
        copy.start()
        eig_in.append(copy)
    small_in = [
        pltpu.make_async_copy(counts_hbm, counts, small_sem.at[1]),
        pltpu.make_async_copy(poles_hbm, poles, small_sem.at[2]),
        pltpu.make_async_copy(weights_hbm, weights, small_sem.at[3]),
        pltpu.make_async_copy(roots_hbm, roots, small_sem.at[4]),
    ]
    for copy in small_in:
        copy.start()

    def send(owner, k, sem, target):
        part = panel.at[owner, pl.ds(k * size, size)]
        return pltpu.make_async_remote_copy(
            src_ref=part, dst_ref=part, send_sem=sem, recv_sem=recv_sem.at[owner, k],
            device_id=target, device_id_type=MESH,
        )

    def arrived(owner, k):
        send(owner, k, partner_sem.at[owner, k], partner).wait_recv()

    def to_partner(owner, k):
        send(owner, k, partner_sem.at[owner, k], partner).start()

    def own_sends(k):
        copies = []
        for j in range(n_fine - 1):
            copies.append(send(me, k, own_sem.at[n_x - 1 + j, k], device_of(x, core, f_of(j))))
        for i in range(n_x - 1):
            copies.append(send(me, k, own_sem.at[i, k], device_of(x_of(i), core, fine)))
        copies.append(send(me, k, partner_sem.at[me, k], partner))
        return copies

    def cross_send(i, j, k):
        first = core == 0
        owner = jnp.where(first, owner_of(x, core, f_of(j)), owner_of(x_of(i), core, fine))
        target = {
            "coarse": jnp.where(first, x_of(i), x) * CORES + core,
            "fine": jnp.where(first, fine, f_of(j)),
        }
        return send(owner, k, cross_sem.at[i * (n_fine - 1) + j, k], target)

    perm_in.wait()
    source = lax.broadcasted_iota(jnp.int32, (columns, LANES), 0)
    for q in range(columns // LANES):
        hit = source == perm[q : q + 1, :]
        select[:, q * LANES : (q + 1) * LANES] = jnp.where(hit, 1.0, 0.0).astype(jnp.bfloat16)

    for k in range(pieces):
        part = pl.ds(k * size, size)
        eig_in[k].wait()
        panel[me, part] = jnp.dot(
            eig[part], select[:, :live], preferred_element_type=jnp.float32
        ).astype(jnp.bfloat16)
        if k == 0:
            pl.semaphore_wait(barrier, n_x + n_fine - 1)
        else:
            for copy in own_sends(k - 1):
                copy.start()
    for copy in small_in:
        copy.wait()
    for copy in own_sends(pieces - 1):
        copy.start()

    width = columns // LANES
    group = 8 // width
    root_row = jnp.concatenate([roots[s : s + 1, :] for s in range(live // LANES)], axis=1)
    within = lax.broadcasted_iota(jnp.int32, (LANES, 1), 0)

    def cauchy_group(t, squares):
        lines = pl.ds(pl.multiple_of(t * 8, 8), 8)
        pole_t = jnp.transpose(poles[lines, :])
        weight_t = jnp.transpose(weights[lines, :])
        for h in range(group):
            block = t * group + h
            count = counts[block]
            for s in range(live // LANES):
                at = h * width + s
                alive = within + s * LANES < count
                factor = jnp.where(alive, weight_t[:, at : at + 1], 0.0)
                value = factor / (pole_t[:, at : at + 1] - root_row)
                squares = squares + jnp.sum(value * value, axis=0, keepdims=True)
                start = pl.multiple_of(block * live + s * LANES, LANES)
                cauchy[pl.ds(start, LANES), :] = value.astype(jnp.bfloat16)
        return squares

    squares = jnp.zeros((1, live), jnp.float32)
    if device_total <= 8:
        for t in range(device_total // group):
            squares = cauchy_group(t, squares)
    else:
        squares = lax.fori_loop(0, device_total // group, cauchy_group, squares)
    scale = 1.0 / jnp.sqrt(squares)

    def product(owner, k):
        start = pl.multiple_of(owner * live, live)
        return jnp.dot(
            panel[owner, pl.ds(k * size, size)], cauchy[pl.ds(start, live), :],
            preferred_element_type=jnp.float32,
        )

    def near(pc):
        return (
            [owner_of(x, pc, fine)]
            + [owner_of(x_of(i), pc, fine) for i in range(n_x - 1)]
            + [owner_of(x, pc, f_of(j)) for j in range(n_fine - 1)]
        )

    crossings = (n_x - 1) * (n_fine - 1)

    def spread(total_steps, body):
        repeat(total_steps, lambda n: body(n // (n_fine - 1), n % (n_fine - 1)))

    def add(owners, k, fresh=False):
        part = pl.ds(k * size, size)
        value = None if fresh else total[part]
        for owner in owners:
            term = product(owner, k)
            value = term if value is None else value + term
        total[part] = value

    def add_near_other(k):
        for owner in near(other_core):
            arrived(owner, k)
        add(near(other_core), k)

    rest_out = pltpu.make_async_copy(rest, out_hbm.at[:, pl.ds(live, columns - live)], rest_sem)

    for k in range(pieces):
        for owner in near(core)[1:]:
            arrived(owner, k)
            to_partner(owner, k)
        spread(crossings, lambda i, j: cross_send(i, j, k).start())
        if k == 0:
            for r in range(pieces):
                part = pl.ds(r * size, size)
                rest[part] = jnp.dot(
                    eig[part], select[:, live:], preferred_element_type=jnp.float32
                ).astype(jnp.bfloat16)
            rest_out.start()
        add(near(core), k, fresh=True)
        if k >= 1:
            add_near_other(k - 1)

    retain = lax.broadcasted_iota(jnp.int32, (1, live), 1) < counts[me]

    def lead_copy(k):
        part = pl.ds(k * size, size)
        return pltpu.make_async_copy(lead.at[part], out_hbm.at[part, pl.ds(0, live)], out_sem.at[k])

    def finish(k):
        part = pl.ds(k * size, size)

        def last(i, j):
            owner = owner_of(x_of(i), other_core, f_of(j))
            arrived(owner, k)
            add([owner], k)

        spread(crossings, last)
        updated = total[part] * scale
        kept = panel[me, part].astype(jnp.float32)
        lead[part] = jnp.where(retain, updated, kept).astype(jnp.bfloat16)
        lead_copy(k).start()

    for k in range(pieces):
        def relay(i, j):
            owner = owner_of(x_of(i), core, f_of(j))
            arrived(owner, k)
            to_partner(owner, k)

        spread(crossings, relay)
        if k == 0:
            add_near_other(pieces - 1)
        spread(crossings, lambda i, j: add([owner_of(x_of(i), core, f_of(j))], k))
        if k >= 1:
            finish(k - 1)
    finish(pieces - 1)

    for k in range(pieces):
        for copy in own_sends(k):
            copy.wait_send()
        for owner in near(core)[1:]:
            send(owner, k, partner_sem.at[owner, k], partner).wait_send()

        def drain(i, j):
            cross_send(i, j, k).wait_send()
            owner = owner_of(x_of(i), core, f_of(j))
            send(owner, k, partner_sem.at[owner, k], partner).wait_send()

        spread(crossings, drain)
    rest_out.wait()
    for k in range(pieces):
        lead_copy(k).wait()


def per_device(n_coarse, n_fine, eigvecs, perm, counts, poles, weights, roots):
    rows, columns = eigvecs.shape
    live = UNDEF_MOST
    device_total = n_coarse * n_fine
    pieces = 4 if device_total <= 8 else 2
    hops = n_coarse // CORES - 1 + n_fine - 1
    crossings = max(1, (n_coarse // CORES - 1) * (n_fine - 1))
    lanes = lambda v: v.reshape(-1, LANES)
    anywhere = pl.BlockSpec(memory_space=pl.ANY)
    return pl.pallas_call(
        functools.partial(merge_kernel, n_coarse, n_fine, pieces),
        out_shape=jax.ShapeDtypeStruct((rows, columns), jnp.bfloat16),
        in_specs=[anywhere] * 6,
        out_specs=anywhere,
        scratch_shapes=[
            pltpu.VMEM((rows, columns), jnp.bfloat16),
            pltpu.VMEM((columns // LANES, LANES), jnp.int32),
            pltpu.SMEM((device_total,), jnp.int32),
            pltpu.VMEM((device_total * columns // LANES, LANES), jnp.float32),
            pltpu.VMEM((device_total * columns // LANES, LANES), jnp.float32),
            pltpu.VMEM((columns // LANES, LANES), jnp.float32),
            pltpu.VMEM((columns, columns), jnp.bfloat16),
            pltpu.VMEM((device_total, rows, live), jnp.bfloat16),
            pltpu.VMEM((device_total * live, live), jnp.bfloat16),
            pltpu.VMEM((rows, live), jnp.float32),
            pltpu.VMEM((rows, columns - live), jnp.bfloat16),
            pltpu.VMEM((rows, live), jnp.bfloat16),
            pltpu.SemaphoreType.DMA((pieces,)),
            pltpu.SemaphoreType.DMA((5,)),
            pltpu.SemaphoreType.DMA((pieces,)),
            pltpu.SemaphoreType.DMA,
            pltpu.SemaphoreType.DMA((device_total, pieces)),
            pltpu.SemaphoreType.DMA((hops, pieces)),
            pltpu.SemaphoreType.DMA((device_total, pieces)),
            pltpu.SemaphoreType.DMA((crossings, pieces)),
        ],
        compiler_params=pltpu.CompilerParams(
            collective_id=0, has_side_effects=True, vmem_limit_bytes=48 * 2**20
        ),
        name="merge",
    )(eigvecs, lanes(perm), counts, lanes(poles), lanes(weights), lanes(roots))


def solution(mesh):
    in_specs = (
        P("rows", ("coarse", "fine")),
        P(("coarse", "fine")),
        P(),
        P(),
        P(),
        P(("coarse", "fine")),
    )
    out_specs = P("rows", ("coarse", "fine"))
    body = functools.partial(per_device, mesh.shape["coarse"], mesh.shape["fine"])
    return jax.shard_map(
        body, mesh=mesh, in_specs=in_specs, out_specs=out_specs, check_vma=False
    )
```

time: 51.2 us -> 21.3 us (0.42)
  the two profiles are of different devices: /device:TPU:0 before, /device:TPU:1 now
where the time goes in v1:
time: 21.3 us; the launch traced here: 20.9 us
  Pallas kernels  16.9 us (79%)
  local copies, waits for them, and re-layouts  3.97 us (19%)
    pallas_call x1, Pallas kernels, per_device(): pl.pallas_call(functools.partial(merge_kernel, n_coarse, n_fine, pieces),...  16.9 us
    unnamed x13, local copies, waits for them, and re-layouts  3.97 us

profile of v1, /device:TPU:1, one launch (start us, length us, event | category | flops | bytes accessed | tf_op | source)
XLA Modules:
  0.0 20.9 jit_solution(7766574015949395084)
XLA Ops:
  0.0 0.0 copy-start.4
  0.0 0.0 copy-start.3
  0.0 0.0 copy-start.5
  0.0 0.7 %copy-done.4 = f32[512]{0:T(512)S(1)} copy-done((f32[512]{0:T(512)S(1)}, f32[512]{0:T(512)}, u32[]{:S(2)}) %copy-start.4) | copy-done | bytes 2072
  0.7 0.0 copy-done.3
  0.7 0.0 copy-done.5
  0.7 0.0 copy-start
  0.7 1.0 %copy-done = bf16[512,512]{1,0:T(8,128)(2,1)S(1)} copy-done((bf16[512,512]{1,0:T(8,128)(2,1)S(1)}, bf16[512,512]{1,0:T(8,128)(2,1)}, u32[]{:S(2)}) %copy-start) | copy-done | bytes 524312
  1.7 0.0 copy-start.1
  1.7 0.7 %copy-done.1 = f32[4096]{0:T(1024)S(1)} copy-done((f32[4096]{0:T(1024)S(1)}, f32[4096]{0:T(1024)}, u32[]{:S(2)}) %copy-start.1) | copy-done | bytes 16408
  2.5 0.0 copy-start.2
  2.5 0.7 %copy-done.2 = f32[4096]{0:T(1024)S(1)} copy-done((f32[4096]{0:T(1024)S(1)}, f32[4096]{0:T(1024)}, u32[]{:S(2)}) %copy-start.2) | copy-done | bytes 16408
  3.2 16.9 %merge.1 = bf16[512,512]{1,0:T(8,128)(2,1)S(1)} custom-call(bf16[512,512]{1,0:T(8,128)(2,1)S(1)} %copy-done, s32[4,128]{1,0:T(4,128)S(1)} %bitcast.6, s32[8]{0:T(128)S(1)} %copy-done.5, f32[32,128]{1,0:T(8,128)S(1)} %bitcast.4, f32[32,128]{1,0:T(8,128)S(1)} %bitcast.5, f32[4,128]{1,0:T(4,128)S(1)} %bitcast.7), custom_call_target="tpu_custom_call" | custom-call | tf_op jit(solution)/shard_map/merge/pallas_call | solution.py:268
  20.1 0.8 %copy.8 = bf16[512,512]{1,0:T(8,128)(2,1)} copy(bf16[512,512]{1,0:T(8,128)(2,1)S(1)} %merge.1) | data formatting | bytes 1048576
Async XLA Ops:
  0.0 0.7 %copy-start.4 = (f32[512]{0:T(512)S(1)}, f32[512]{0:T(512)}, u32[]{:S(2)}) copy-start(f32[512]{0:T(512)} %param.11) | copy-start | bytes 6148
  0.0 0.7 %copy-start.3 = (s32[512]{0:T(512)S(1)}, s32[512]{0:T(512)}, u32[]{:S(2)}) copy-start(s32[512]{0:T(512)} %param.7) | copy-start | bytes 6148
  0.0 0.7 %copy-start.5 = (s32[8]{0:T(128)S(1)}, s32[8]{0:T(128)}, u32[]{:S(2)}) copy-start(s32[8]{0:T(128)} %counts_hbm.1) | copy-start | bytes 100
  0.7 1.0 %copy-start = (bf16[512,512]{1,0:T(8,128)(2,1)S(1)}, bf16[512,512]{1,0:T(8,128)(2,1)}, u32[]{:S(2)}) copy-start(bf16[512,512]{1,0:T(8,128)(2,1)} %eig_hbm.1) | copy-start | bytes 1572868
  1.7 0.7 %copy-start.1 = (f32[4096]{0:T(1024)S(1)}, f32[4096]{0:T(1024)}, u32[]{:S(2)}) copy-start(f32[4096]{0:T(1024)} %param.9) | copy-start | bytes 49156
  2.5 0.7 %copy-start.2 = (f32[4096]{0:T(1024)S(1)}, f32[4096]{0:T(1024)}, u32[]{:S(2)}) copy-start(f32[4096]{0:T(1024)} %param.10) | copy-start | bytes 49156

commit v2 on v1

--- a/solution.py
+++ b/solution.py
@@ -22,9 +22,9 @@
 
 
 def merge_kernel(
-    n_coarse, n_fine, pieces, eig_hbm, perm_hbm, counts_hbm, poles_hbm, weights_hbm, roots_hbm, out_hbm,
-    eig, perm, counts, poles, weights, roots, select, panel, cauchy, total, rest, lead,
-    in_sem, small_sem, out_sem, rest_sem, recv_sem, own_sem, partner_sem, cross_sem,
+    n_coarse, n_fine, pieces, eig_hbm, perm_hbm, counts_hbm, poles_hbm, weights_hbm, roots_hbm, out,
+    eig, perm, counts, poles, weights, roots, select, panel, cauchy, total,
+    in_sem, small_sem, recv_sem, own_sem, partner_sem, cross_sem,
 ):
     rows, columns = eig.shape
     live = UNDEF_MOST
@@ -187,8 +187,6 @@
             arrived(owner, k)
         add(near(other_core), k)
 
-    rest_out = pltpu.make_async_copy(rest, out_hbm.at[:, pl.ds(live, columns - live)], rest_sem)
-
     for k in range(pieces):
         for owner in near(core)[1:]:
             arrived(owner, k)
@@ -197,19 +195,14 @@
         if k == 0:
             for r in range(pieces):
                 part = pl.ds(r * size, size)
-                rest[part] = jnp.dot(
+                out[part, live:] = jnp.dot(
                     eig[part], select[:, live:], preferred_element_type=jnp.float32
                 ).astype(jnp.bfloat16)
-            rest_out.start()
         add(near(core), k, fresh=True)
         if k >= 1:
             add_near_other(k - 1)
 
     retain = lax.broadcasted_iota(jnp.int32, (1, live), 1) < counts[me]
-
-    def lead_copy(k):
-        part = pl.ds(k * size, size)
-        return pltpu.make_async_copy(lead.at[part], out_hbm.at[part, pl.ds(0, live)], out_sem.at[k])
 
     def finish(k):
         part = pl.ds(k * size, size)
@@ -222,8 +215,7 @@
         spread(crossings, last)
         updated = total[part] * scale
         kept = panel[me, part].astype(jnp.float32)
-        lead[part] = jnp.where(retain, updated, kept).astype(jnp.bfloat16)
-        lead_copy(k).start()
+        out[part, :live] = jnp.where(retain, updated, kept).astype(jnp.bfloat16)
 
     for k in range(pieces):
         def relay(i, j):
@@ -251,9 +243,6 @@
             send(owner, k, partner_sem.at[owner, k], partner).wait_send()
 
         spread(crossings, drain)
-    rest_out.wait()
-    for k in range(pieces):
-        lead_copy(k).wait()
 
 
 def per_device(n_coarse, n_fine, eigvecs, perm, counts, poles, weights, roots):
@@ -264,12 +253,13 @@
     hops = n_coarse // CORES - 1 + n_fine - 1
     crossings = max(1, (n_coarse // CORES - 1) * (n_fine - 1))
     lanes = lambda v: v.reshape(-1, LANES)
-    anywhere = pl.BlockSpec(memory_space=pl.ANY)
+    operands = [eigvecs, lanes(perm), counts, lanes(poles), lanes(weights), lanes(roots)]
+    anywhere = pl.BlockSpec(memory_space=pltpu.HBM)
     return pl.pallas_call(
         functools.partial(merge_kernel, n_coarse, n_fine, pieces),
         out_shape=jax.ShapeDtypeStruct((rows, columns), jnp.bfloat16),
         in_specs=[anywhere] * 6,
-        out_specs=anywhere,
+        out_specs=pl.BlockSpec(memory_space=pltpu.VMEM),
         scratch_shapes=[
             pltpu.VMEM((rows, columns), jnp.bfloat16),
             pltpu.VMEM((columns // LANES, LANES), jnp.int32),
@@ -281,12 +271,8 @@
             pltpu.VMEM((device_total, rows, live), jnp.bfloat16),
             pltpu.VMEM((device_total * live, live), jnp.bfloat16),
             pltpu.VMEM((rows, live), jnp.float32),
-            pltpu.VMEM((rows, columns - live), jnp.bfloat16),
-            pltpu.VMEM((rows, live), jnp.bfloat16),
             pltpu.SemaphoreType.DMA((pieces,)),
             pltpu.SemaphoreType.DMA((5,)),
-            pltpu.SemaphoreType.DMA((pieces,)),
-            pltpu.SemaphoreType.DMA,
             pltpu.SemaphoreType.DMA((device_total, pieces)),
             pltpu.SemaphoreType.DMA((hops, pieces)),
             pltpu.SemaphoreType.DMA((device_total, pieces)),
@@ -296,7 +282,7 @@
             collective_id=0, has_side_effects=True, vmem_limit_bytes=48 * 2**20
         ),
         name="merge",
-    )(eigvecs, lanes(perm), counts, lanes(poles), lanes(weights), lanes(roots))
+    )(*[pltpu.with_memory_space_constraint(v, pltpu.HBM) for v in operands])
 
 
 def solution(mesh):

time: 21.3 us -> 17.9 us (0.84)
  the two profiles are of different devices: /device:TPU:1 before, /device:TPU:0 now
where the time goes in v2:
time: 17.9 us; the launch traced here: 17.7 us
  Pallas kernels  16.9 us (94%)
  local copies, waits for them, and re-layouts  0.8 us (4%)
    pallas_call x1, Pallas kernels, per_device(): pl.pallas_call(functools.partial(merge_kernel, n_coarse, n_fine, pieces),...  16.9 us
    unnamed x1, local copies, waits for them, and re-layouts  0.8 us

profile of v2, /device:TPU:0, one launch (start us, length us, event | category | flops | bytes accessed | tf_op | source)
XLA Modules:
  0.0 17.7 jit_solution(7086082275253287798)
XLA Ops:
  0.0 16.9 %merge.1 = bf16[512,512]{1,0:T(8,128)(2,1)S(1)} custom-call(bf16[512,512]{1,0:T(8,128)(2,1)} %eig_hbm.1, s32[4,128]{1,0:T(4,128)} %bitcast.6, s32[8]{0:T(128)} %counts_hbm.1, f32[32,128]{1,0:T(8,128)} %bitcast.4, f32[32,128]{1,0:T(8,128)} %bitcast.5, f32[4,128]{1,0:T(4,128)} %bitcast.7), custom_call_target="tpu_custom_call" | custom-call | tf_op jit(solution)/shard_map/merge/pallas_call | solution.py:258
  16.9 0.8 %copy.8 = bf16[512,512]{1,0:T(8,128)(2,1)} copy(bf16[512,512]{1,0:T(8,128)(2,1)S(1)} %merge.1) | data formatting | bytes 1048576

commit v3 on v2

--- a/solution.py
+++ b/solution.py
@@ -85,29 +85,46 @@
     def to_partner(owner, k):
         send(owner, k, partner_sem.at[owner, k], partner).start()
 
-    def own_sends(k):
-        copies = []
-        for j in range(n_fine - 1):
-            copies.append(send(me, k, own_sem.at[n_x - 1 + j, k], device_of(x, core, f_of(j))))
-        for i in range(n_x - 1):
-            copies.append(send(me, k, own_sem.at[i, k], device_of(x_of(i), core, fine)))
-        copies.append(send(me, k, partner_sem.at[me, k], partner))
-        return copies
+    n_lead, n_trail = n_fine - 1, n_x - 1
+    balanced = n_lead == n_trail
+
+    def choose(k, a, b):
+        return jnp.where(core == k % CORES, a, b) if balanced else a
+
+    def lead_owner(j, k):
+        return choose(k, owner_of(x, core, f_of(j)), owner_of(x_of(j), core, fine))
+
+    def trail_owner(i, k):
+        return choose(k, owner_of(x_of(i), core, fine), owner_of(x, core, f_of(i)))
+
+    def lead_target(j, k):
+        return {"coarse": choose(k, x, x_of(j)) * CORES + core, "fine": choose(k, f_of(j), fine)}
+
+    def trail_target(i, k):
+        return {"coarse": choose(k, x_of(i), x) * CORES + core, "fine": choose(k, fine, f_of(i))}
+
+    def lead_send(j, k):
+        return send(me, k, own_sem.at[j, k], lead_target(j, k))
+
+    def trail_send(i, k):
+        return send(me, k, own_sem.at[n_lead + i, k], trail_target(i, k))
 
     def cross_send(i, j, k):
-        first = core == 0
-        owner = jnp.where(first, owner_of(x, core, f_of(j)), owner_of(x_of(i), core, fine))
-        target = {
-            "coarse": jnp.where(first, x_of(i), x) * CORES + core,
-            "fine": jnp.where(first, fine, f_of(j)),
-        }
-        return send(owner, k, cross_sem.at[i * (n_fine - 1) + j, k], target)
+        return send(lead_owner(j, k), k, cross_sem.at[i * n_lead + j, k], trail_target(i, k))
+
+    def early_sends(k):
+        for j in range(n_lead):
+            lead_send(j, k).start()
+        to_partner(me, k)
+
+    def build_select(low, high):
+        source = lax.broadcasted_iota(jnp.int32, (columns, LANES), 0)
+        for q in range(low // LANES, high // LANES):
+            hit = source == perm[q : q + 1, :]
+            select[:, q * LANES : (q + 1) * LANES] = jnp.where(hit, 1.0, 0.0).astype(jnp.bfloat16)
 
     perm_in.wait()
-    source = lax.broadcasted_iota(jnp.int32, (columns, LANES), 0)
-    for q in range(columns // LANES):
-        hit = source == perm[q : q + 1, :]
-        select[:, q * LANES : (q + 1) * LANES] = jnp.where(hit, 1.0, 0.0).astype(jnp.bfloat16)
+    build_select(0, live)
 
     for k in range(pieces):
         part = pl.ds(k * size, size)
@@ -117,13 +134,13 @@
         ).astype(jnp.bfloat16)
         if k == 0:
             pl.semaphore_wait(barrier, n_x + n_fine - 1)
-        else:
-            for copy in own_sends(k - 1):
-                copy.start()
+            early_sends(0)
+        elif k >= 2:
+            early_sends(k - 1)
     for copy in small_in:
         copy.wait()
-    for copy in own_sends(pieces - 1):
-        copy.start()
+    if pieces > 1:
+        early_sends(pieces - 1)
 
     width = columns // LANES
     group = 8 // width
@@ -162,14 +179,7 @@
             preferred_element_type=jnp.float32,
         )
 
-    def near(pc):
-        return (
-            [owner_of(x, pc, fine)]
-            + [owner_of(x_of(i), pc, fine) for i in range(n_x - 1)]
-            + [owner_of(x, pc, f_of(j)) for j in range(n_fine - 1)]
-        )
-
-    crossings = (n_x - 1) * (n_fine - 1)
+    crossings = n_lead * n_trail
 
     def spread(total_steps, body):
         repeat(total_steps, lambda n: body(n // (n_fine - 1), n % (n_fine - 1)))
@@ -182,33 +192,52 @@
             value = term if value is None else value + term
         total[part] = value
 
-    def add_near_other(k):
-        for owner in near(other_core):
-            arrived(owner, k)
-        add(near(other_core), k)
-
-    for k in range(pieces):
-        for owner in near(core)[1:]:
-            arrived(owner, k)
-            to_partner(owner, k)
-        spread(crossings, lambda i, j: cross_send(i, j, k).start())
+    def near_group(pc, k, fresh=False):
+        add([owner_of(x, pc, fine)] + [lead_owner_of(pc, j, k) for j in range(n_lead)], k, fresh)
+
+    def lead_owner_of(pc, j, k):
+        if pc is core or not balanced:
+            return pc_owner(lead_owner(j, k), pc)
+        return pc_owner(trail_owner(j, k), pc)
+
+    def trail_owner_of(pc, i, k):
+        if pc is core or not balanced:
+            return pc_owner(trail_owner(i, k), pc)
+        return pc_owner(lead_owner(i, k), pc)
+
+    def pc_owner(owner, pc):
+        return owner if pc is core else owner + (pc - core) * n_fine
+
+    def far_owner(pc, i, j):
+        return owner_of(x_of(i), pc, f_of(j))
+
+    for k in range(pieces):
+        for j in range(n_lead):
+            arrived(lead_owner(j, k), k)
+            for i in range(n_trail):
+                trail_send(i, k).start() if j == 0 else None
+                cross_send(i, j, k).start()
+            to_partner(lead_owner(j, k), k)
         if k == 0:
+            build_select(live, columns)
             for r in range(pieces):
                 part = pl.ds(r * size, size)
                 out[part, live:] = jnp.dot(
                     eig[part], select[:, live:], preferred_element_type=jnp.float32
                 ).astype(jnp.bfloat16)
-        add(near(core), k, fresh=True)
-        if k >= 1:
-            add_near_other(k - 1)
+        near_group(core, k, fresh=True)
 
     retain = lax.broadcasted_iota(jnp.int32, (1, live), 1) < counts[me]
 
     def finish(k):
         part = pl.ds(k * size, size)
+        for i in range(n_trail):
+            arrived(trail_owner_of(other_core, i, k), k)
+        if n_trail > 0:
+            add([trail_owner_of(other_core, i, k) for i in range(n_trail)], k)
 
         def last(i, j):
-            owner = owner_of(x_of(i), other_core, f_of(j))
+            owner = far_owner(other_core, i, j)
             arrived(owner, k)
             add([owner], k)
 
@@ -218,28 +247,38 @@
         out[part, :live] = jnp.where(retain, updated, kept).astype(jnp.bfloat16)
 
     for k in range(pieces):
+        for i in range(n_trail):
+            arrived(trail_owner(i, k), k)
+            to_partner(trail_owner(i, k), k)
+
         def relay(i, j):
-            owner = owner_of(x_of(i), core, f_of(j))
-            arrived(owner, k)
-            to_partner(owner, k)
+            arrived(far_owner(core, i, j), k)
+            to_partner(far_owner(core, i, j), k)
 
         spread(crossings, relay)
-        if k == 0:
-            add_near_other(pieces - 1)
-        spread(crossings, lambda i, j: add([owner_of(x_of(i), core, f_of(j))], k))
+        arrived(owner_of(x, other_core, fine), k)
+        for j in range(n_lead):
+            arrived(lead_owner_of(other_core, j, k), k)
+        near_group(other_core, k)
+        if n_trail > 0:
+            add([trail_owner(i, k) for i in range(n_trail)], k)
+        spread(crossings, lambda i, j: add([far_owner(core, i, j)], k))
         if k >= 1:
             finish(k - 1)
     finish(pieces - 1)
 
     for k in range(pieces):
-        for copy in own_sends(k):
-            copy.wait_send()
-        for owner in near(core)[1:]:
-            send(owner, k, partner_sem.at[owner, k], partner).wait_send()
+        for j in range(n_lead):
+            lead_send(j, k).wait_send()
+            send(lead_owner(j, k), k, partner_sem.at[lead_owner(j, k), k], partner).wait_send()
+        for i in range(n_trail):
+            trail_send(i, k).wait_send()
+            send(trail_owner(i, k), k, partner_sem.at[trail_owner(i, k), k], partner).wait_send()
+        send(me, k, partner_sem.at[me, k], partner).wait_send()
 
         def drain(i, j):
             cross_send(i, j, k).wait_send()
-            owner = owner_of(x_of(i), core, f_of(j))
+            owner = far_owner(core, i, j)
             send(owner, k, partner_sem.at[owner, k], partner).wait_send()
 
         spread(crossings, drain)

time: 17.9 us -> 17.6 us (0.983)
  Pallas kernels: 16.9 us -> 16.6 us
    pallas_call x1, Pallas kernels: 16.9 us -> 16.6 us  [per_device(): pl.pallas_call(functools.partial(merge_kernel, n_coarse, n_fine, pieces),...]
where the time goes in v3:
time: 17.6 us; the launch traced here: 17.4 us
  Pallas kernels  16.6 us (94%)
  local copies, waits for them, and re-layouts  0.8 us (5%)
    pallas_call x1, Pallas kernels, per_device(): pl.pallas_call(functools.partial(merge_kernel, n_coarse, n_fine, pieces),...  16.6 us
    unnamed x1, local copies, waits for them, and re-layouts  0.8 us

profile of v3, /device:TPU:0, one launch (start us, length us, event | category | flops | bytes accessed | tf_op | source)
XLA Modules:
  0.0 17.4 jit_solution(10831291043700112126)
XLA Ops:
  0.0 16.6 %merge.1 = bf16[512,512]{1,0:T(8,128)(2,1)S(1)} custom-call(bf16[512,512]{1,0:T(8,128)(2,1)} %eig_hbm.1, s32[4,128]{1,0:T(4,128)} %bitcast.6, s32[8]{0:T(128)} %counts_hbm.1, f32[32,128]{1,0:T(8,128)} %bitcast.4, f32[32,128]{1,0:T(8,128)} %bitcast.5, f32[4,128]{1,0:T(4,128)} %bitcast.7), custom_call_target="tpu_custom_call" | custom-call | tf_op jit(solution)/shard_map/merge/pallas_call | solution.py:297
  16.6 0.8 %copy.8 = bf16[512,512]{1,0:T(8,128)(2,1)} copy(bf16[512,512]{1,0:T(8,128)(2,1)S(1)} %merge.1) | data formatting | bytes 1048576

commit v4 on v3

v4 whole, which is shorter than its diff:
```python
import functools

import jax
import jax.numpy as jnp
from jax import lax
from jax.experimental import pallas as pl
from jax.experimental.pallas import tpu as pltpu
from jax.sharding import PartitionSpec as P

UNDEF_MOST = 256
LANES = 128
CORES = 2
MESH = pl.DeviceIdType.MESH


def repeat(total, body):
    if total <= 8:
        for i in range(total):
            body(i)
    else:
        lax.fori_loop(0, total, lambda i, c: (body(i), c)[1], 0)


def merge_kernel(
    n_coarse, n_fine, pieces, eig_hbm, perm_hbm, counts_hbm, poles_hbm, weights_hbm, roots_hbm, out,
    eig, perm, counts, poles, weights, roots, select, panel, cauchy, total,
    peer_roots, peer_cauchy, partial, incoming,
    in_sem, small_sem, recv_sem, own_sem, partner_sem, sum_send_sem, sum_recv_sem, root_send_sem, root_recv_sem,
):
    rows, columns = eig.shape
    live = UNDEF_MOST
    device_total = n_coarse * n_fine
    n_x = n_coarse // CORES
    size = rows // pieces
    coarse = lax.axis_index("coarse")
    fine = lax.axis_index("fine")
    x = coarse // CORES
    core = lax.rem(coarse, CORES)
    other_core = 1 - core

    def owner_of(px, pc, pf):
        return (px * CORES + pc) * n_fine + pf

    def device_of(px, pc, pf):
        return {"coarse": px * CORES + pc, "fine": pf}

    me = owner_of(x, core, fine)
    x_of = lambda i: lax.rem(x + 1 + i, n_x)
    f_of = lambda j: lax.rem(fine + 1 + j, n_fine)
    partner = device_of(x, other_core, fine)

    barrier = pltpu.get_barrier_semaphore()
    pl.semaphore_signal(barrier, inc=1, device_id=partner, device_id_type=MESH)
    for i in range(n_x - 1):
        pl.semaphore_signal(barrier, inc=1, device_id=device_of(x_of(i), core, fine), device_id_type=MESH)
    for j in range(n_fine - 1):
        pl.semaphore_signal(barrier, inc=1, device_id=device_of(x, core, f_of(j)), device_id_type=MESH)

    perm_in = pltpu.make_async_copy(perm_hbm, perm, small_sem.at[0])
    perm_in.start()
    eig_in = []
    for k in range(pieces):
        part = pl.ds(k * size, size)
        copy = pltpu.make_async_copy(eig_hbm.at[part], eig.at[part], in_sem.at[k])
        copy.start()
        eig_in.append(copy)
    small_in = [
        pltpu.make_async_copy(counts_hbm, counts, small_sem.at[1]),
        pltpu.make_async_copy(poles_hbm, poles, small_sem.at[2]),
        pltpu.make_async_copy(weights_hbm, weights, small_sem.at[3]),
    ]
    roots_in = pltpu.make_async_copy(roots_hbm, roots, small_sem.at[4])
    roots_in.start()
    for copy in small_in:
        copy.start()

    def send(owner, k, sem, target):
        part = panel.at[owner, pl.ds(k * size, size)]
        return pltpu.make_async_remote_copy(
            src_ref=part, dst_ref=part, send_sem=sem, recv_sem=recv_sem.at[owner, k],
            device_id=target, device_id_type=MESH,
        )

    def arrived(owner, k):
        send(owner, k, partner_sem.at[owner, k], partner).wait_recv()

    def to_partner(owner, k):
        send(owner, k, partner_sem.at[owner, k], partner).start()

    balanced = n_x == n_fine
    over_fine = lambda k: not balanced or k % 2 == 0
    x_peers = [(x_of(i), fine) for i in range(n_x - 1)]
    f_peers = [(x, f_of(j)) for j in range(n_fine - 1)]

    def gather_peers(k):
        return f_peers if over_fine(k) else x_peers

    def sum_peers(k):
        return x_peers if over_fine(k) else f_peers

    def peer_owner(peer, pc):
        return owner_of(peer[0], pc, peer[1])

    def gather_send(n, k):
        px, pf = gather_peers(k)[n]
        return send(me, k, own_sem.at[n, k], device_of(px, core, pf))

    def early_sends(k):
        for n in range(len(gather_peers(k))):
            gather_send(n, k).start()
        to_partner(me, k)

    def sum_send(n, k):
        part = pl.ds(k * size, size)
        peers = sum_peers(k)
        px, pf = peers[n]
        slot = len(peers) - 1 - n
        return pltpu.make_async_remote_copy(
            src_ref=partial.at[n, part], dst_ref=incoming.at[slot, part],
            send_sem=sum_send_sem.at[n, k], recv_sem=sum_recv_sem.at[slot, k],
            device_id=device_of(px, core, pf), device_id_type=MESH,
        )

    root_peers = x_peers + (f_peers if balanced else [])

    def root_send(n):
        px, pf = root_peers[n]
        base, count = (0, n_x - 1) if n < n_x - 1 else (n_x - 1, n_fine - 1)
        slot = base + count - 1 - (n - base)
        return pltpu.make_async_remote_copy(
            src_ref=roots, dst_ref=peer_roots.at[slot],
            send_sem=root_send_sem.at[n], recv_sem=root_recv_sem.at[slot],
            device_id=device_of(px, core, pf), device_id_type=MESH,
        )

    def build_select(low, high):
        source = lax.broadcasted_iota(jnp.int32, (columns, LANES), 0)
        for q in range(low // LANES, high // LANES):
            hit = source == perm[q : q + 1, :]
            select[:, q * LANES : (q + 1) * LANES] = jnp.where(hit, 1.0, 0.0).astype(jnp.bfloat16)

    perm_in.wait()
    build_select(0, live)

    for k in range(pieces):
        part = pl.ds(k * size, size)
        eig_in[k].wait()
        panel[me, part] = jnp.dot(
            eig[part], select[:, :live], preferred_element_type=jnp.float32
        ).astype(jnp.bfloat16)
        if k == 0:
            pl.semaphore_wait(barrier, n_x + n_fine - 1)
            roots_in.wait()
            for n in range(len(root_peers)):
                root_send(n).start()
            early_sends(0)
        elif k >= 2:
            early_sends(k - 1)
    for copy in small_in:
        copy.wait()
    if pieces > 1:
        early_sends(pieces - 1)

    width = columns // LANES
    group = 8 // width
    as_row = lambda v: jnp.concatenate([v[n : n + 1, :] for n in range(live // LANES)], axis=1)
    root_row = as_row(roots)
    within = lax.broadcasted_iota(jnp.int32, (LANES, 1), 0)

    def cauchy_group(t, squares):
        lines = pl.ds(pl.multiple_of(t * 8, 8), 8)
        pole_t = jnp.transpose(poles[lines, :])
        weight_t = jnp.transpose(weights[lines, :])
        for h in range(group):
            block = t * group + h
            count = counts[block]
            for s in range(live // LANES):
                at = h * width + s
                alive = within + s * LANES < count
                factor = jnp.where(alive, weight_t[:, at : at + 1], 0.0)
                value = factor / (pole_t[:, at : at + 1] - root_row)
                squares = squares + jnp.sum(value * value, axis=0, keepdims=True)
                start = pl.multiple_of(block * live + s * LANES, LANES)
                cauchy[pl.ds(start, LANES), :] = value.astype(jnp.bfloat16)
        return squares

    def peer_block(slot, row, block):
        lines = pl.ds(pl.multiple_of(block // group * 8, 8), 8)
        pole_t = jnp.transpose(poles[lines, :])
        weight_t = jnp.transpose(weights[lines, :])
        h = lax.rem(block, group)
        count = counts[block]
        for s in range(live // LANES):
            pole, weight = pole_t[:, s : s + 1], weight_t[:, s : s + 1]
            for other in range(1, group):
                at = other * width + s
                pole = jnp.where(h == other, pole_t[:, at : at + 1], pole)
                weight = jnp.where(h == other, weight_t[:, at : at + 1], weight)
            factor = jnp.where(within + s * LANES < count, weight, 0.0)
            value = factor / (pole - row)
            start = pl.multiple_of(block * live + s * LANES, LANES)
            peer_cauchy[slot, pl.ds(start, LANES), :] = value.astype(jnp.bfloat16)

    def gathered(k, pc):
        return [owner_of(x, pc, fine)] + [peer_owner(p, pc) for p in gather_peers(k)]

    for n in range(len(root_peers)):
        root_send(n).wait_recv()
    for n in range(len(root_peers)):
        row = as_row(peer_roots.at[n])
        if n < n_x - 1:
            repeat(CORES * n_fine, lambda b: peer_block(n, row, x * CORES * n_fine + b))
        else:
            repeat(CORES * n_x, lambda b: peer_block(n, row, b * n_fine + fine))

    def product(source, owner, k):
        start = pl.multiple_of(owner * live, live)
        return jnp.dot(
            panel[owner, pl.ds(k * size, size)], source[pl.ds(start, live), :],
            preferred_element_type=jnp.float32,
        )

    def block_sum(source, k):
        value = None
        for owner in gathered(k, core) + gathered(k, other_core):
            term = product(source, owner, k)
            value = term if value is None else value + term
        return value

    def relay(k):
        for owner in gathered(k, core)[1:]:
            arrived(owner, k)
            to_partner(owner, k)

    def rest_piece(k):
        part = pl.ds(k * size, size)
        out[part, live:] = jnp.dot(
            eig[part], select[:, live:], preferred_element_type=jnp.float32
        ).astype(jnp.bfloat16)

    def partials(k):
        part = pl.ds(k * size, size)
        for owner in gathered(k, other_core):
            arrived(owner, k)
        base = 0 if over_fine(k) else n_x - 1
        for n in range(len(sum_peers(k))):
            partial[n, part] = block_sum(peer_cauchy.at[base + n], k).astype(jnp.bfloat16)
        rest_piece(k)
        for n in range(len(sum_peers(k))):
            sum_send(n, k).start()

    retain = lax.broadcasted_iota(jnp.int32, (1, live), 1) < counts[me]

    def finish(k):
        part = pl.ds(k * size, size)
        value = total[part]
        for n in range(len(sum_peers(k))):
            sum_send(n, k).wait_recv()
        for n in range(len(sum_peers(k))):
            value = value + incoming[n, part].astype(jnp.float32)
        updated = value * scale
        kept = panel[me, part].astype(jnp.float32)
        out[part, :live] = jnp.where(retain, updated, kept).astype(jnp.bfloat16)

    build_select(live, columns)
    ahead = min(2, pieces)
    for k in range(ahead):
        relay(k)
    for k in range(pieces):
        partials(k)
        if k + ahead < pieces:
            relay(k + ahead)
    squares = jnp.zeros((1, live), jnp.float32)
    if device_total <= 8:
        for t in range(device_total // group):
            squares = cauchy_group(t, squares)
    else:
        squares = lax.fori_loop(0, device_total // group, cauchy_group, squares)
    scale = 1.0 / jnp.sqrt(squares)

    for k in range(pieces):
        total[pl.ds(k * size, size)] = block_sum(cauchy, k)
    for k in range(pieces):
        finish(k)

    for n in range(len(root_peers)):
        root_send(n).wait_send()
    for k in range(pieces):
        for n in range(len(gather_peers(k))):
            gather_send(n, k).wait_send()
        for owner in gathered(k, core):
            send(owner, k, partner_sem.at[owner, k], partner).wait_send()
        for n in range(len(sum_peers(k))):
            sum_send(n, k).wait_send()


def per_device(n_coarse, n_fine, eigvecs, perm, counts, poles, weights, roots):
    rows, columns = eigvecs.shape
    live = UNDEF_MOST
    device_total = n_coarse * n_fine
    pieces = 4 if device_total <= 8 else 2
    n_x = n_coarse // CORES
    hops = max(n_x, n_fine) - 1
    sums = n_x - 1
    row_sets = n_x - 1 + (n_fine - 1 if n_x == n_fine else 0)
    lanes = lambda v: v.reshape(-1, LANES)
    operands = [eigvecs, lanes(perm), counts, lanes(poles), lanes(weights), lanes(roots)]
    anywhere = pl.BlockSpec(memory_space=pltpu.HBM)
    return pl.pallas_call(
        functools.partial(merge_kernel, n_coarse, n_fine, pieces),
        out_shape=jax.ShapeDtypeStruct((rows, columns), jnp.bfloat16),
        in_specs=[anywhere] * 6,
        out_specs=pl.BlockSpec(memory_space=pltpu.VMEM),
        scratch_shapes=[
            pltpu.VMEM((rows, columns), jnp.bfloat16),
            pltpu.VMEM((columns // LANES, LANES), jnp.int32),
            pltpu.SMEM((device_total,), jnp.int32),
            pltpu.VMEM((device_total * columns // LANES, LANES), jnp.float32),
            pltpu.VMEM((device_total * columns // LANES, LANES), jnp.float32),
            pltpu.VMEM((columns // LANES, LANES), jnp.float32),
            pltpu.VMEM((columns, columns), jnp.bfloat16),
            pltpu.VMEM((device_total, rows, live), jnp.bfloat16),
            pltpu.VMEM((device_total * live, live), jnp.bfloat16),
            pltpu.VMEM((rows, live), jnp.float32),
            pltpu.VMEM((row_sets, columns // LANES, LANES), jnp.float32),
            pltpu.VMEM((row_sets, device_total * live, live), jnp.bfloat16),
            pltpu.VMEM((sums, rows, live), jnp.bfloat16),
            pltpu.VMEM((sums, rows, live), jnp.bfloat16),
            pltpu.SemaphoreType.DMA((pieces,)),
            pltpu.SemaphoreType.DMA((5,)),
            pltpu.SemaphoreType.DMA((device_total, pieces)),
            pltpu.SemaphoreType.DMA((hops, pieces)),
            pltpu.SemaphoreType.DMA((device_total, pieces)),
            pltpu.SemaphoreType.DMA((sums, pieces)),
            pltpu.SemaphoreType.DMA((sums, pieces)),
            pltpu.SemaphoreType.DMA((row_sets,)),
            pltpu.SemaphoreType.DMA((row_sets,)),
        ],
        compiler_params=pltpu.CompilerParams(
            collective_id=0, has_side_effects=True, vmem_limit_bytes=48 * 2**20
        ),
        name="merge",
    )(*[pltpu.with_memory_space_constraint(v, pltpu.HBM) for v in operands])


def solution(mesh):
    in_specs = (
        P("rows", ("coarse", "fine")),
        P(("coarse", "fine")),
        P(),
        P(),
        P(),
        P(("coarse", "fine")),
    )
    out_specs = P("rows", ("coarse", "fine"))
    body = functools.partial(per_device, mesh.shape["coarse"], mesh.shape["fine"])
    return jax.shard_map(
        body, mesh=mesh, in_specs=in_specs, out_specs=out_specs, check_vma=False
    )
```

time: 17.6 us -> 16.1 us (0.915)
  Pallas kernels: 16.6 us -> 15.1 us
    pallas_call x1, Pallas kernels: 16.6 us -> 15.1 us  [per_device(): pl.pallas_call(functools.partial(merge_kernel, n_coarse, n_fine, pieces),...]
where the time goes in v4:
time: 16.1 us; the launch traced here: 15.9 us
  Pallas kernels  15.1 us (94%)
  local copies, waits for them, and re-layouts  0.8 us (5%)
    pallas_call x1, Pallas kernels, per_device(): pl.pallas_call(functools.partial(merge_kernel, n_coarse, n_fine, pieces),...  15.1 us
    unnamed x1, local copies, waits for them, and re-layouts  0.8 us

profile of v4, /device:TPU:0, one launch (start us, length us, event | category | flops | bytes accessed | tf_op | source)
XLA Modules:
  0.0 15.9 jit_solution(8114012373941512046)
XLA Ops:
  0.0 15.1 %merge.1 = bf16[512,512]{1,0:T(8,128)(2,1)S(1)} custom-call(bf16[512,512]{1,0:T(8,128)(2,1)} %eig_hbm.1, s32[4,128]{1,0:T(4,128)} %bitcast.6, s32[8]{0:T(128)} %counts_hbm.1, f32[32,128]{1,0:T(8,128)} %bitcast.4, f32[32,128]{1,0:T(8,128)} %bitcast.5, f32[4,128]{1,0:T(4,128)} %bitcast.7), custom_call_target="tpu_custom_call" | custom-call | tf_op jit(solution)/shard_map/merge/pallas_call | solution.py:309
  15.1 0.8 %copy.8 = bf16[512,512]{1,0:T(8,128)(2,1)} copy(bf16[512,512]{1,0:T(8,128)(2,1)S(1)} %merge.1) | data formatting | bytes 1048576

commit v5 on v4

--- a/solution.py
+++ b/solution.py
@@ -204,14 +204,18 @@
     def gathered(k, pc):
         return [owner_of(x, pc, fine)] + [peer_owner(p, pc) for p in gather_peers(k)]
 
+    build_select(live, columns)
     for n in range(len(root_peers)):
         root_send(n).wait_recv()
-    for n in range(len(root_peers)):
+    def peer_panel(n):
         row = as_row(peer_roots.at[n])
         if n < n_x - 1:
             repeat(CORES * n_fine, lambda b: peer_block(n, row, x * CORES * n_fine + b))
         else:
             repeat(CORES * n_x, lambda b: peer_block(n, row, b * n_fine + fine))
+
+    for n in range(n_x - 1):
+        peer_panel(n)
 
     def product(source, owner, k):
         start = pl.multiple_of(owner * live, live)
@@ -262,10 +266,11 @@
         kept = panel[me, part].astype(jnp.float32)
         out[part, :live] = jnp.where(retain, updated, kept).astype(jnp.bfloat16)
 
-    build_select(live, columns)
-    ahead = min(2, pieces)
+    ahead = min(4, pieces)
     for k in range(ahead):
         relay(k)
+    for n in range(n_x - 1, len(root_peers)):
+        peer_panel(n)
     for k in range(pieces):
         partials(k)
         if k + ahead < pieces:

time: 16.1 us -> 15.9 us (0.988)
  no operation moved by 1% of the time
where the time goes in v5:
time: 15.9 us; the launch traced here: 15.8 us
  Pallas kernels  15 us (94%)
  local copies, waits for them, and re-layouts  0.8 us (5%)
    pallas_call x1, Pallas kernels, per_device(): pl.pallas_call(functools.partial(merge_kernel, n_coarse, n_fine, pieces),...  15 us
    unnamed x1, local copies, waits for them, and re-layouts  0.8 us

profile of v5, /device:TPU:0, one launch (start us, length us, event | category | flops | bytes accessed | tf_op | source)
XLA Modules:
  0.0 15.8 jit_solution(12098764238179042050)
XLA Ops:
  0.0 15.0 %merge.1 = bf16[512,512]{1,0:T(8,128)(2,1)S(1)} custom-call(bf16[512,512]{1,0:T(8,128)(2,1)} %eig_hbm.1, s32[4,128]{1,0:T(4,128)} %bitcast.6, s32[8]{0:T(128)} %counts_hbm.1, f32[32,128]{1,0:T(8,128)} %bitcast.4, f32[32,128]{1,0:T(8,128)} %bitcast.5, f32[4,128]{1,0:T(4,128)} %bitcast.7), custom_call_target="tpu_custom_call" | custom-call | tf_op jit(solution)/shard_map/merge/pallas_call | solution.py:314
  15.0 0.8 %copy.8 = bf16[512,512]{1,0:T(8,128)(2,1)} copy(bf16[512,512]{1,0:T(8,128)(2,1)S(1)} %merge.1) | data formatting | bytes 1048576
